TPU v7x, 512 devices: a whole 4x4x16 slice. The times are simulated.
512 devices in a mesh: ctx: 64 (over y, z), head: 8 (over x, core).
Axes of the slice: x: 4, y: 4, z: 16, core: 2. Of those that a mesh axis runs over, the one named last changes fastest.
Arguments:
- queries: bfloat16 [32768, 4096], P(('ctx', 'head')), may hold values from -12 to 12
- keys: bfloat16 [32768, 1024], P(('ctx', 'head')), may hold values from -12 to 12
- values: bfloat16 [32768, 1024], P(('ctx', 'head')), may hold values from -6 to 6
- doc_lengths: int32 [16], replicated, may hold values from 1 to 4096, 32768 in all
- piece_owner: int32 [64, 64], P('ctx'), may hold values from 0 to 63, each once within a row
Outputs:
- owned: bfloat16 [32768, 4096], P('ctx', 'head')
Inputs may be any that keep to these rules, and one draw needn't show every extreme that they name: Each row of piece_owner is a permutation of 0 .. 63. doc_lengths sum to 32768, and the largest equals 4096.
All inputs are finite; a program needn't handle non-finite values.
Results may differ from a plain program's by a relative error of at most 0.0033.
Values may be sent and summed in bfloat16 or wider, within the bound.
A program may use at most 64 MiB of HBM per device.

v0:
```python
import math
import jax
import jax.numpy as jnp
from jax import lax
from jax.sharding import PartitionSpec as P

HD = 128
QPK = 4
MOST = 4096
masked_score = -1e30


def passed_along(value, axis, steps):
    count = lax.axis_size(axis)
    leading, last = (max(0, -steps), min(count, count - steps))
    return lax.ppermute(value, axis, [(source, source + steps) for source in range(leading, last)])


def doc_index(positions, doc_lengths):
    doc_ends = jnp.cumsum(doc_lengths)
    return jnp.sum((positions[:, None] >= doc_ends[None, :]).astype(jnp.int32), axis=1)


def per_device(queries, keys, values, doc_lengths, piece_owner):
    query_rows, key_rows, value_rows = (
        lax.all_to_all(queries, "head", split_axis=1, concat_axis=0, tiled=True),
        lax.all_to_all(keys, "head", split_axis=1, concat_axis=0, tiled=True),
        lax.all_to_all(values, "head", split_axis=1, concat_axis=0, tiled=True),
    )
    tokens_here = query_rows.shape[0]
    groups = key_rows.shape[1] // HD
    features = query_rows.shape[1]
    reach_back = (MOST - 1) // tokens_here + 1
    score_scale = 1.0 / math.sqrt(HD)
    ctx_place = lax.axis_index("ctx")
    offsets = jnp.arange(tokens_here, dtype=jnp.int32)
    query_position = ctx_place * tokens_here + offsets
    query_ids = doc_index(query_position, doc_lengths)
    paired = jnp.stack([key_rows, value_rows])
    shards = [paired]
    for distance in range(1, reach_back + 1):
        shards.append(passed_along(paired, "ctx", distance))
    key_positions = []
    key_ids = []
    for distance in range(reach_back + 1):
        shard_position = (ctx_place - distance) * tokens_here + offsets
        key_positions.append(shard_position)
        key_ids.append(doc_index(shard_position, doc_lengths))
    block_rows = 512
    block_count = tokens_here // block_rows
    query_split = query_rows.reshape(block_count, block_rows, groups, QPK, HD)
    position_split = query_position.reshape(block_count, block_rows)
    ids_split = query_ids.reshape(block_count, block_rows)

    def attend(operands):
        query_block, position_block, ids_block = operands
        row_top = jnp.full((block_rows, groups, QPK), masked_score, jnp.float32)
        row_total = jnp.zeros((block_rows, groups, QPK), jnp.float32)
        weighted = jnp.zeros((block_rows, groups, QPK, HD), jnp.float32)
        carry_state = (row_top, row_total, weighted)
        for distance in range(reach_back + 1):
            shard_pair = shards[distance]
            shard_keys = shard_pair[0].reshape(tokens_here, groups, HD)
            shard_values = shard_pair[1].reshape(tokens_here, groups, HD)
            live_pairs = (
                (key_positions[distance][None, :] >= 0)
                & (key_positions[distance][None, :] <= position_block[:, None])
                & (key_ids[distance][None, :] == ids_block[:, None])
            )

            def update(
                state_now, shard_keys=shard_keys, shard_values=shard_values, live_pairs=live_pairs
            ):
                old_top, old_total, old_weighted = state_now
                live_mask = live_pairs[:, None, None, :]
                scores = (
                    jnp.einsum(
                        "qgjd,kgd->qgjk",
                        query_block,
                        shard_keys,
                        preferred_element_type=jnp.float32,
                    )
                    * score_scale
                )
                scores = jnp.where(live_mask, scores, masked_score)
                new_top = jnp.maximum(old_top, jnp.max(scores, axis=-1))
                factor = jnp.exp(old_top - new_top)
                weights = jnp.where(live_mask, jnp.exp(scores - new_top[..., None]), 0.0)
                new_total = old_total * factor + jnp.sum(weights, axis=-1)
                new_weighted = old_weighted * factor[..., None] + jnp.einsum(
                    "qgjk,kgd->qgjd",
                    weights.astype(jnp.bfloat16),
                    shard_values,
                    preferred_element_type=jnp.float32,
                )
                return (new_top, new_total, new_weighted)

            carry_state = update(carry_state)
        final_top, final_total, final_weighted = carry_state
        result = final_weighted / final_total[..., None]
        return result.astype(jnp.bfloat16).reshape(block_rows, groups * QPK * HD)

    attended = lax.map(attend, (query_split, position_split, ids_split)).reshape(
        tokens_here, features
    )
    ctx_count = lax.axis_size("ctx")
    piece_rows = tokens_here // ctx_count
    owner_row = piece_owner[0]
    slot_index = jnp.arange(ctx_count, dtype=jnp.int32)
    matches = owner_row[:, None] == slot_index[None, :]
    inverse = jnp.sum(jnp.where(matches, slot_index[:, None], 0), axis=0)
    pieces = attended.reshape(ctx_count, piece_rows, features)
    ordered = jnp.take(pieces, inverse, axis=0)
    received = lax.all_to_all(ordered, "ctx", split_axis=0, concat_axis=0, tiled=True)
    return received.reshape(tokens_here, features)


def solution(mesh):
    return jax.shard_map(
        per_device,
        mesh=mesh,
        in_specs=(
            P(("ctx", "head"), None),
            P(("ctx", "head"), None),
            P(("ctx", "head"), None),
            P(),
            P("ctx", None),
        ),
        out_specs=P("ctx", "head"),
        check_vma=False,
    )
```

profile of v0, /device:TPU:4, one launch (start us, length us, event | category | flops | bytes accessed | tf_op | source)
XLA Modules:
  0.0 324.6 jit_solution(12941780340591550754)
XLA Ops:
  0.0 0.9 copy-done
  0.9 0.7 copy_bitcast_fusion.2
  1.6 9.1 %all-to-all-start = ((bf16[64,8,128]{2,0,1:T(8,128)(2,1)}), bf16[64,8,128]{2,0,1:T(8,128)(2,1)S(1)}, u32[]{:S(2)}, u32[]{:S(2)}) async-start(bf16[64,8,128]{2,0,1:T(8,128)(2,1)} %copy_bitcast_fusion.2), calls=%async_computation | async-start | bytes 262144 | tf_op jit(solution)/shard_map/all_to_all | solution.py:27
  10.8 0.7 select_reduce_fusion
  11.6 0.7 copy.73
  12.4 0.1 reduce.18
  12.5 1.6 copy_bitcast_fusion.1
  14.1 0.1 convert_reduce_fusion
  14.2 2.7 compare_and_fusion.8
  17.0 0.0 all-to-all-done
  17.0 4.8 %all-to-all-start.2 = ((bf16[64,8,128]{2,0,1:T(8,128)(2,1)}), bf16[64,8,128]{2,0,1:T(8,128)(2,1)S(1)}, u32[]{:S(2)}, u32[]{:S(2)}) async-start(bf16[64,8,128]{2,0,1:T(8,128)(2,1)} %copy_bitcast_fusion.1), calls=%async_computation.2 | async-start | bytes 262144 | tf_op jit(solution)/shard_map/all_to_all | solution.py:28
  21.8 1.9 copy.187
  23.7 1.5 all-to-all-done.2
  25.2 6.1 %all-to-all-start.1 = ((bf16[64,8,512]{2,0,1:T(8,128)(2,1)}), bf16[64,8,512]{2,0,1:T(8,128)(2,1)S(1)}, u32[]{:S(2)}, u32[]{:S(2)}) async-start(bf16[64,8,512]{2,0,1:T(8,128)(2,1)} %bitcast.463), calls=%async_computation.1 | async-start | bytes 1048576 | tf_op jit(solution)/shard_map/all_to_all | solution.py:26
  31.3 1.2 compare_and_fusion.7
  32.5 0.7 pad_maximum_fusion
  33.3 12.1 %collective-permute-start.7 = (bf16[2,512,128]{2,1,0:T(8,128)(2,1)}, bf16[2,512,128]{2,1,0:T(8,128)(2,1)}, u32[]{:S(2)}, u32[]{:S(2)}) collective-permute-start(bf16[2,512,128]{2,1,0:T(8,128)(2,1)} %pad_maximum_fusion), channel_id=1, source_target_pairs={{0,64},{8,72},{16,80},{24,88},{32,96},{40,104},{48,112},{56,120},{... | collective-permute-start | bytes 786440 | tf_op jit(solution)/shard_map/ppermute | solution.py:16
  45.3 6.4 %collective-permute-start.6 = (bf16[2,512,128]{2,1,0:T(8,128)(2,1)}, bf16[2,512,128]{2,1,0:T(8,128)(2,1)}, u32[]{:S(2)}, u32[]{:S(2)}) collective-permute-start(bf16[2,512,128]{2,1,0:T(8,128)(2,1)} %pad_maximum_fusion), channel_id=1, source_target_pairs={{0,56},{8,64},{16,72},{24,80},{32,88},{40,96},{48,104},{56,112},{6... | collective-permute-start | bytes 786440 | tf_op jit(solution)/shard_map/ppermute | solution.py:16
  51.7 4.7 %collective-permute-start.5 = (bf16[2,512,128]{2,1,0:T(8,128)(2,1)}, bf16[2,512,128]{2,1,0:T(8,128)(2,1)}, u32[]{:S(2)}, u32[]{:S(2)}) collective-permute-start(bf16[2,512,128]{2,1,0:T(8,128)(2,1)} %pad_maximum_fusion), channel_id=1, source_target_pairs={{0,48},{8,56},{16,64},{24,72},{32,80},{40,88},{48,96},{56,104},{64... | collective-permute-start | bytes 786440 | tf_op jit(solution)/shard_map/ppermute | solution.py:16
  56.4 8.6 %collective-permute-start.4 = (bf16[2,512,128]{2,1,0:T(8,128)(2,1)}, bf16[2,512,128]{2,1,0:T(8,128)(2,1)}, u32[]{:S(2)}, u32[]{:S(2)}) collective-permute-start(bf16[2,512,128]{2,1,0:T(8,128)(2,1)} %pad_maximum_fusion), channel_id=1, source_target_pairs={{0,40},{8,48},{16,56},{24,64},{32,72},{40,80},{48,88},{56,96},{64,... | collective-permute-start | bytes 786440 | tf_op jit(solution)/shard_map/ppermute | solution.py:16
  65.0 3.4 %collective-permute-start.1 = (bf16[2,512,128]{2,1,0:T(8,128)(2,1)}, bf16[2,512,128]{2,1,0:T(8,128)(2,1)}, u32[]{:S(2)}, u32[]{:S(2)}) collective-permute-start(bf16[2,512,128]{2,1,0:T(8,128)(2,1)} %pad_maximum_fusion), channel_id=1, source_target_pairs={{0,16},{8,24},{16,32},{24,40},{32,48},{40,56},{48,64},{56,72},{64,... | collective-permute-start | bytes 786440 | tf_op jit(solution)/shard_map/ppermute | solution.py:16
  68.4 0.1 reshape.1350
  68.5 0.9 fusion
  69.4 109.8 %collective-permute-done.1 = bf16[2,512,128]{2,1,0:T(8,128)(2,1)} collective-permute-done((bf16[2,512,128]{2,1,0:T(8,128)(2,1)}, bf16[2,512,128]{2,1,0:T(8,128)(2,1)}, u32[]{:S(2)}, u32[]{:S(2)}) %collective-permute-start.1) | collective-permute-done | bytes 262176 | tf_op jit(solution)/shard_map/ppermute | solution.py:16
  179.2 5.8 %collective-permute-start.2 = (bf16[2,512,128]{2,1,0:T(8,128)(2,1)}, bf16[2,512,128]{2,1,0:T(8,128)(2,1)S(1)}, u32[]{:S(2)}, u32[]{:S(2)}) collective-permute-start(bf16[2,512,128]{2,1,0:T(8,128)(2,1)} %pad_maximum_fusion), channel_id=1, source_target_pairs={{0,24},{8,32},{16,40},{24,48},{32,56},{40,64},{48,72},{56,80},{64,... | collective-permute-start | bytes 786440 | tf_op jit(solution)/shard_map/ppermute | solution.py:16
  185.0 1.8 fusion.2
  186.8 10.9 %collective-permute-done.2 = bf16[2,512,128]{2,1,0:T(8,128)(2,1)S(1)} collective-permute-done((bf16[2,512,128]{2,1,0:T(8,128)(2,1)}, bf16[2,512,128]{2,1,0:T(8,128)(2,1)S(1)}, u32[]{:S(2)}, u32[]{:S(2)}) %collective-permute-start.2) | collective-permute-done | bytes 262176 | tf_op jit(solution)/shard_map/ppermute | solution.py:16
  197.7 11.1 %collective-permute-start.3 = (bf16[2,512,128]{2,1,0:T(8,128)(2,1)}, bf16[2,512,128]{2,1,0:T(8,128)(2,1)S(1)}, u32[]{:S(2)}, u32[]{:S(2)}) collective-permute-start(bf16[2,512,128]{2,1,0:T(8,128)(2,1)} %pad_maximum_fusion), channel_id=1, source_target_pairs={{0,32},{8,40},{16,48},{24,56},{32,64},{40,72},{48,80},{56,88},{64,... | collective-permute-start | bytes 786440 | tf_op jit(solution)/shard_map/ppermute | solution.py:16
  208.8 0.9 fusion.3
  209.7 7.8 %collective-permute-done.3 = bf16[2,512,128]{2,1,0:T(8,128)(2,1)S(1)} collective-permute-done((bf16[2,512,128]{2,1,0:T(8,128)(2,1)}, bf16[2,512,128]{2,1,0:T(8,128)(2,1)S(1)}, u32[]{:S(2)}, u32[]{:S(2)}) %collective-permute-start.3) | collective-permute-done | bytes 262176 | tf_op jit(solution)/shard_map/ppermute | solution.py:16
  217.5 9.1 %collective-permute-start = (bf16[2,512,128]{2,1,0:T(8,128)(2,1)}, bf16[2,512,128]{2,1,0:T(8,128)(2,1)S(1)}, u32[]{:S(2)}, u32[]{:S(2)}) collective-permute-start(bf16[2,512,128]{2,1,0:T(8,128)(2,1)} %pad_maximum_fusion), channel_id=1, source_target_pairs={{0,8},{8,16},{16,24},{24,32},{32,40},{40,48},{48,56},{56,64},{64,7... | collective-permute-start | bytes 786440 | tf_op jit(solution)/shard_map/ppermute | solution.py:16
  226.6 0.9 fusion.4
  227.5 1.8 fusion.5
  229.3 1.8 fusion.6
  231.1 5.2 %collective-permute-done = bf16[2,512,128]{2,1,0:T(8,128)(2,1)S(1)} collective-permute-done((bf16[2,512,128]{2,1,0:T(8,128)(2,1)}, bf16[2,512,128]{2,1,0:T(8,128)(2,1)S(1)}, u32[]{:S(2)}, u32[]{:S(2)}) %collective-permute-start) | collective-permute-done | bytes 262176 | tf_op jit(solution)/shard_map/ppermute | solution.py:16
  236.3 0.9 fusion.1
  237.2 1.8 fusion.7
  239.0 1.8 fusion.8
  240.9 1.1 fusion.9
  241.9 1.1 fusion.25
  243.0 1.0 fusion.23
  244.0 1.0 fusion.21
  245.1 1.0 fusion.19
  246.1 1.1 fusion.17
  247.2 1.3 fusion.15
  248.5 1.0 fusion.13
  249.5 1.0 fusion.11
  250.6 0.1 multiply_add_fusion
  250.6 2.1 fusion.93
  252.7 2.4 fusion.66
  255.1 2.4 fusion.69
  257.5 0.0 copy-start.7
  257.5 2.4 fusion.72
  259.9 1.5 fusion.75
  261.4 1.5 fusion.78
  262.9 2.4 fusion.81
  265.4 3.1 fusion.141
  268.5 2.9 divide_convert_fusion
  271.4 0.4 copy.111
  271.9 0.2 reshape_reshape.3
  272.1 0.6 gather_fusion
  272.7 0.1 broadcast_select_fusion
  272.8 50.9 %all_to_all.53 = bf16[64,8,512]{2,1,0:T(8,128)(2,1)S(1)} all-to-all(bf16[64,8,512]{2,1,0:T(8,128)(2,1)S(1)} %broadcast_select_fusion), channel_id=1, replica_groups=mesh['ctx'=64,'head'=8] {'ctx'}, dimensions={0} | all-to-all | bytes 1048576 | tf_op jit(solution)/shard_map/all_to_all | solution.py:114
  323.8 0.8 copy.189
  (34 shorter events, 0.2 us)
Async XLA Ops:
  0.0 0.9 copy-start
  1.6 15.4 %all-to-all-start = ((bf16[64,8,128]{2,0,1:T(8,128)(2,1)}), bf16[64,8,128]{2,0,1:T(8,128)(2,1)S(1)}, u32[]{:S(2)}, u32[]{:S(2)}) async-start(bf16[64,8,128]{2,0,1:T(8,128)(2,1)} %copy_bitcast_fusion.2), calls=%async_computation | async-start | bytes 262144 | tf_op jit(solution)/shard_map/all_to_all | solution.py:27
  17.0 8.2 %all-to-all-start.2 = ((bf16[64,8,128]{2,0,1:T(8,128)(2,1)}), bf16[64,8,128]{2,0,1:T(8,128)(2,1)S(1)}, u32[]{:S(2)}, u32[]{:S(2)}) async-start(bf16[64,8,128]{2,0,1:T(8,128)(2,1)} %copy_bitcast_fusion.1), calls=%async_computation.2 | async-start | bytes 262144 | tf_op jit(solution)/shard_map/all_to_all | solution.py:28
  25.2 43.2 %all-to-all-start.1 = ((bf16[64,8,512]{2,0,1:T(8,128)(2,1)}), bf16[64,8,512]{2,0,1:T(8,128)(2,1)S(1)}, u32[]{:S(2)}, u32[]{:S(2)}) async-start(bf16[64,8,512]{2,0,1:T(8,128)(2,1)} %bitcast.463), calls=%async_computation.1 | async-start | bytes 1048576 | tf_op jit(solution)/shard_map/all_to_all | solution.py:26
  33.3 205.8 %collective-permute-start.7 = (bf16[2,512,128]{2,1,0:T(8,128)(2,1)}, bf16[2,512,128]{2,1,0:T(8,128)(2,1)}, u32[]{:S(2)}, u32[]{:S(2)}) collective-permute-start(bf16[2,512,128]{2,1,0:T(8,128)(2,1)} %pad_maximum_fusion), channel_id=1, source_target_pairs={{0,64},{8,72},{16,80},{24,88},{32,96},{40,104},{48,112},{56,120},{... | collective-permute-start | bytes 786440 | tf_op jit(solution)/shard_map/ppermute | solution.py:16
  45.3 191.9 %collective-permute-start.6 = (bf16[2,512,128]{2,1,0:T(8,128)(2,1)}, bf16[2,512,128]{2,1,0:T(8,128)(2,1)}, u32[]{:S(2)}, u32[]{:S(2)}) collective-permute-start(bf16[2,512,128]{2,1,0:T(8,128)(2,1)} %pad_maximum_fusion), channel_id=1, source_target_pairs={{0,56},{8,64},{16,72},{24,80},{32,88},{40,96},{48,104},{56,112},{6... | collective-permute-start | bytes 786440 | tf_op jit(solution)/shard_map/ppermute | solution.py:16
  51.7 177.6 %collective-permute-start.5 = (bf16[2,512,128]{2,1,0:T(8,128)(2,1)}, bf16[2,512,128]{2,1,0:T(8,128)(2,1)}, u32[]{:S(2)}, u32[]{:S(2)}) collective-permute-start(bf16[2,512,128]{2,1,0:T(8,128)(2,1)} %pad_maximum_fusion), channel_id=1, source_target_pairs={{0,48},{8,56},{16,64},{24,72},{32,80},{40,88},{48,96},{56,104},{64... | collective-permute-start | bytes 786440 | tf_op jit(solution)/shard_map/ppermute | solution.py:16
  56.4 171.1 %collective-permute-start.4 = (bf16[2,512,128]{2,1,0:T(8,128)(2,1)}, bf16[2,512,128]{2,1,0:T(8,128)(2,1)}, u32[]{:S(2)}, u32[]{:S(2)}) collective-permute-start(bf16[2,512,128]{2,1,0:T(8,128)(2,1)} %pad_maximum_fusion), channel_id=1, source_target_pairs={{0,40},{8,48},{16,56},{24,64},{32,72},{40,80},{48,88},{56,96},{64,... | collective-permute-start | bytes 786440 | tf_op jit(solution)/shard_map/ppermute | solution.py:16
  65.0 114.2 %collective-permute-start.1 = (bf16[2,512,128]{2,1,0:T(8,128)(2,1)}, bf16[2,512,128]{2,1,0:T(8,128)(2,1)}, u32[]{:S(2)}, u32[]{:S(2)}) collective-permute-start(bf16[2,512,128]{2,1,0:T(8,128)(2,1)} %pad_maximum_fusion), channel_id=1, source_target_pairs={{0,16},{8,24},{16,32},{24,40},{32,48},{40,56},{48,64},{56,72},{64,... | collective-permute-start | bytes 786440 | tf_op jit(solution)/shard_map/ppermute | solution.py:16
  179.2 18.5 %collective-permute-start.2 = (bf16[2,512,128]{2,1,0:T(8,128)(2,1)}, bf16[2,512,128]{2,1,0:T(8,128)(2,1)S(1)}, u32[]{:S(2)}, u32[]{:S(2)}) collective-permute-start(bf16[2,512,128]{2,1,0:T(8,128)(2,1)} %pad_maximum_fusion), channel_id=1, source_target_pairs={{0,24},{8,32},{16,40},{24,48},{32,56},{40,64},{48,72},{56,80},{64,... | collective-permute-start | bytes 786440 | tf_op jit(solution)/shard_map/ppermute | solution.py:16
  197.7 29.8 %copy-start.4 = (bf16[2,512,128]{2,1,0:T(8,128)(2,1)}, bf16[2,512,128]{2,1,0:T(8,128)(2,1)S(1)}, u32[]{:S(2)}) copy-start(bf16[2,512,128]{2,1,0:T(8,128)(2,1)S(1)} %collective-permute-done.2) | copy-start | bytes 786436
  197.7 19.8 %collective-permute-start.3 = (bf16[2,512,128]{2,1,0:T(8,128)(2,1)}, bf16[2,512,128]{2,1,0:T(8,128)(2,1)S(1)}, u32[]{:S(2)}, u32[]{:S(2)}) collective-permute-start(bf16[2,512,128]{2,1,0:T(8,128)(2,1)} %pad_maximum_fusion), channel_id=1, source_target_pairs={{0,32},{8,40},{16,48},{24,56},{32,64},{40,72},{48,80},{56,88},{64,... | collective-permute-start | bytes 786440 | tf_op jit(solution)/shard_map/ppermute | solution.py:16
  217.5 11.8 %copy-start.6 = (bf16[2,512,128]{2,1,0:T(8,128)(2,1)}, bf16[2,512,128]{2,1,0:T(8,128)(2,1)S(1)}, u32[]{:S(2)}) copy-start(bf16[2,512,128]{2,1,0:T(8,128)(2,1)S(1)} %collective-permute-done.3) | copy-start | bytes 786436
  217.5 18.8 %collective-permute-start = (bf16[2,512,128]{2,1,0:T(8,128)(2,1)}, bf16[2,512,128]{2,1,0:T(8,128)(2,1)S(1)}, u32[]{:S(2)}, u32[]{:S(2)}) collective-permute-start(bf16[2,512,128]{2,1,0:T(8,128)(2,1)} %pad_maximum_fusion), channel_id=1, source_target_pairs={{0,8},{8,16},{16,24},{24,32},{32,40},{40,48},{48,56},{56,64},{64,7... | collective-permute-start | bytes 786440 | tf_op jit(solution)/shard_map/ppermute | solution.py:16
  226.6 2.8 copy-start.1
  236.3 2.7 copy-start.2
  257.5 2.4 copy-start.7
  259.9 1.5 copy-start.5
  262.9 2.4 copy-start.3
where the time goes:
time: 325 us
  waiting for transfers between devices  135 us (42%)
  starting transfers between devices  81.1 us (25%)
  blocking collectives  50.9 us (16%)
  matrix products  33.3 us (10%)
  other arithmetic  15.7 us (5%)
  local copies, waits for them, and re-layouts  7.92 us (2%)
    ppermute x8, waiting for transfers between devices, passed_along(): lax.ppermute(value, axis, [(source, source + steps) for source in range(l...  134 us
    ppermute x8, starting transfers between devices, passed_along(): lax.ppermute(value, axis, [(source, source + steps) for source in range(l...  61.1 us
    all_to_all x1, blocking collectives, per_device(): lax.all_to_all(ordered, 'ctx', split_axis=0, concat_axis=0, tiled=True)  50.9 us
    dot_general x9, matrix products, update(): jnp.einsum('qgjk,kgd->qgjd', weights.astype(jnp.bfloat16), shard_values,...  20.7 us
    dot_general x9, matrix products, update(): jnp.einsum('qgjd,kgd->qgjk', query_block, shard_keys, preferred_element_t...  12.6 us
    reduce_sum x9, other arithmetic, update(): new_total = old_total * factor + jnp.sum(weights, axis=-1)  9.67 us
    all_to_all x1, starting transfers between devices, per_device(): lax.all_to_all(keys, 'head', split_axis=1, concat_axis=0, tiled=True)  9.15 us
  transfers between devices with their start and end apart: 11, of which 5 were waited for; matrix products, arithmetic and copies ran while one was open for 6% of the time, Pallas kernels for 0%

commit v1 on v0

--- a/solution.py
+++ b/solution.py
@@ -24,7 +24,10 @@
 def per_device(queries, keys, values, doc_lengths, piece_owner):
     query_rows, key_rows, value_rows = (
         lax.all_to_all(queries, "head", split_axis=1, concat_axis=0, tiled=True),
-        lax.all_to_all(keys, "head", split_axis=1, concat_axis=0, tiled=True),
+        jnp.concatenate(
+            lax.all_to_all(jnp.stack(jnp.split(keys, lax.axis_size("head"), axis=1)), "head", 0, 0),
+            axis=0,
+        ),
         lax.all_to_all(values, "head", split_axis=1, concat_axis=0, tiled=True),
     )
     tokens_here = query_rows.shape[0]

time: 325 us -> 335 us (1.031)
  local copies, waits for them, and re-layouts: 7.92 us -> 16.9 us
    unnamed x17 -> x24, local copies, waits for them, and re-layouts: 1.73 us -> 10.9 us
    all_to_all x1, starting transfers between devices: 9.15 us -> 4.8 us  [per_device(): lax.all_to_all(jnp.stack(jnp.split(keys, lax.axis_size('head'), axis=1)),...]
    all_to_all x1, starting transfers between devices: 4.8 us -> 9.15 us  [per_device(): lax.all_to_all(values, 'head', split_axis=1, concat_axis=0, tiled=True)]
  transfers between devices with their start and end apart: 11 -> 11, of which waited for: 5 -> 5; matrix products, arithmetic and copies ran while one was open for 6% -> 9% of each run, Pallas kernels for 0% -> 0%
where the time goes in v1:
time: 335 us; the launch traced here: 334 us
  waiting for transfers between devices  135 us (40%)
  starting transfers between devices  81.1 us (24%)
  blocking collectives  50.9 us (15%)
  matrix products  33.4 us (10%)
  local copies, waits for them, and re-layouts  16.9 us (5%)
  other arithmetic  15.7 us (5%)
    ppermute x8, waiting for transfers between devices, passed_along(): lax.ppermute(value, axis, [(source, source + steps) for source in range(l...  134 us
    ppermute x8, starting transfers between devices, passed_along(): lax.ppermute(value, axis, [(source, source + steps) for source in range(l...  61.1 us
    all_to_all x1, blocking collectives, per_device(): lax.all_to_all(ordered, 'ctx', split_axis=0, concat_axis=0, tiled=True)  50.9 us
    dot_general x9, matrix products, update(): jnp.einsum('qgjk,kgd->qgjd', weights.astype(jnp.bfloat16), shard_values,...  20.8 us
    dot_general x9, matrix products, update(): jnp.einsum('qgjd,kgd->qgjk', query_block, shard_keys, preferred_element_t...  12.6 us
    unnamed x24, local copies, waits for them, and re-layouts  10.9 us
    reduce_sum x9, other arithmetic, update(): new_total = old_total * factor + jnp.sum(weights, axis=-1)  9.65 us
    all_to_all x1, starting transfers between devices, per_device(): lax.all_to_all(values, 'head', split_axis=1, concat_axis=0, tiled=True)  9.15 us
  transfers between devices with their start and end apart: 11, of which 5 were waited for; matrix products, arithmetic and copies ran while one was open for 9% of the time, Pallas kernels for 0%

profile of v1, /device:TPU:4, one launch (start us, length us, event | category | flops | bytes accessed | tf_op | source)
XLA Modules:
  0.0 333.6 jit_solution(10061666812885193452)
XLA Ops:
  0.0 0.9 copy-done
  0.9 0.7 copy_bitcast_fusion.1
  1.6 9.1 %all-to-all-start.2 = ((bf16[64,8,128]{2,0,1:T(8,128)(2,1)}), bf16[64,8,128]{2,0,1:T(8,128)(2,1)S(1)}, u32[]{:S(2)}, u32[]{:S(2)}) async-start(bf16[64,8,128]{2,0,1:T(8,128)(2,1)} %copy_bitcast_fusion.1), calls=%async_computation.2 | async-start | bytes 262144 | tf_op jit(solution)/shard_map/all_to_all | solution.py:31
  10.8 0.7 select_reduce_fusion
  11.6 0.7 copy.71
  12.5 1.3 constant_dynamic-update-slice_fusion.7
  13.8 1.3 constant_dynamic-update-slice_fusion.6
  15.1 1.3 constant_dynamic-update-slice_fusion.5
  16.4 1.3 constant_dynamic-update-slice_fusion.4
  17.8 1.3 constant_dynamic-update-slice_fusion.3
  19.1 1.3 constant_dynamic-update-slice_fusion.2
  20.4 1.3 constant_dynamic-update-slice_fusion.1
  21.7 1.3 constant_dynamic-update-slice_fusion
  23.2 2.7 compare_and_fusion.8
  25.9 4.8 %all-to-all-start = ((bf16[8,64,128]{2,1,0:T(8,128)(2,1)}), bf16[8,64,128]{2,1,0:T(8,128)(2,1)S(1)}, u32[]{:S(2)}, u32[]{:S(2)}) async-start(bf16[8,64,128]{2,1,0:T(8,128)(2,1)} %constant_dynamic-update-slice_fusion), calls=%async_computation | async-start | bytes 262144 | tf_op jit(solution)/shard_map/all_to_all | solution.py:28
  30.7 1.9 copy.182
  32.6 1.5 all-to-all-done
  34.1 6.1 %all-to-all-start.1 = ((bf16[64,8,512]{2,0,1:T(8,128)(2,1)}), bf16[64,8,512]{2,0,1:T(8,128)(2,1)S(1)}, u32[]{:S(2)}, u32[]{:S(2)}) async-start(bf16[64,8,512]{2,0,1:T(8,128)(2,1)} %bitcast.471), calls=%async_computation.1 | async-start | bytes 1048576 | tf_op jit(solution)/shard_map/all_to_all | solution.py:26
  40.3 1.2 compare_and_fusion.7
  41.5 0.7 pad_maximum_fusion
  42.2 12.1 %collective-permute-start.7 = (bf16[2,512,128]{2,1,0:T(8,128)(2,1)}, bf16[2,512,128]{2,1,0:T(8,128)(2,1)}, u32[]{:S(2)}, u32[]{:S(2)}) collective-permute-start(bf16[2,512,128]{2,1,0:T(8,128)(2,1)} %pad_maximum_fusion), channel_id=1, source_target_pairs={{0,64},{8,72},{16,80},{24,88},{32,96},{40,104},{48,112},{56,120},{... | collective-permute-start | bytes 786440 | tf_op jit(solution)/shard_map/ppermute | solution.py:16
  54.3 6.4 %collective-permute-start.6 = (bf16[2,512,128]{2,1,0:T(8,128)(2,1)}, bf16[2,512,128]{2,1,0:T(8,128)(2,1)}, u32[]{:S(2)}, u32[]{:S(2)}) collective-permute-start(bf16[2,512,128]{2,1,0:T(8,128)(2,1)} %pad_maximum_fusion), channel_id=1, source_target_pairs={{0,56},{8,64},{16,72},{24,80},{32,88},{40,96},{48,104},{56,112},{6... | collective-permute-start | bytes 786440 | tf_op jit(solution)/shard_map/ppermute | solution.py:16
  60.7 4.7 %collective-permute-start.5 = (bf16[2,512,128]{2,1,0:T(8,128)(2,1)}, bf16[2,512,128]{2,1,0:T(8,128)(2,1)}, u32[]{:S(2)}, u32[]{:S(2)}) collective-permute-start(bf16[2,512,128]{2,1,0:T(8,128)(2,1)} %pad_maximum_fusion), channel_id=1, source_target_pairs={{0,48},{8,56},{16,64},{24,72},{32,80},{40,88},{48,96},{56,104},{64... | collective-permute-start | bytes 786440 | tf_op jit(solution)/shard_map/ppermute | solution.py:16
  65.3 8.6 %collective-permute-start.4 = (bf16[2,512,128]{2,1,0:T(8,128)(2,1)}, bf16[2,512,128]{2,1,0:T(8,128)(2,1)}, u32[]{:S(2)}, u32[]{:S(2)}) collective-permute-start(bf16[2,512,128]{2,1,0:T(8,128)(2,1)} %pad_maximum_fusion), channel_id=1, source_target_pairs={{0,40},{8,48},{16,56},{24,64},{32,72},{40,80},{48,88},{56,96},{64,... | collective-permute-start | bytes 786440 | tf_op jit(solution)/shard_map/ppermute | solution.py:16
  74.0 3.4 %collective-permute-start.1 = (bf16[2,512,128]{2,1,0:T(8,128)(2,1)}, bf16[2,512,128]{2,1,0:T(8,128)(2,1)}, u32[]{:S(2)}, u32[]{:S(2)}) collective-permute-start(bf16[2,512,128]{2,1,0:T(8,128)(2,1)} %pad_maximum_fusion), channel_id=1, source_target_pairs={{0,16},{8,24},{16,32},{24,40},{32,48},{40,56},{48,64},{56,72},{64,... | collective-permute-start | bytes 786440 | tf_op jit(solution)/shard_map/ppermute | solution.py:16
  77.5 0.9 fusion
  78.4 109.8 %collective-permute-done.1 = bf16[2,512,128]{2,1,0:T(8,128)(2,1)} collective-permute-done((bf16[2,512,128]{2,1,0:T(8,128)(2,1)}, bf16[2,512,128]{2,1,0:T(8,128)(2,1)}, u32[]{:S(2)}, u32[]{:S(2)}) %collective-permute-start.1) | collective-permute-done | bytes 262176 | tf_op jit(solution)/shard_map/ppermute | solution.py:16
  188.2 5.8 %collective-permute-start.2 = (bf16[2,512,128]{2,1,0:T(8,128)(2,1)}, bf16[2,512,128]{2,1,0:T(8,128)(2,1)S(1)}, u32[]{:S(2)}, u32[]{:S(2)}) collective-permute-start(bf16[2,512,128]{2,1,0:T(8,128)(2,1)} %pad_maximum_fusion), channel_id=1, source_target_pairs={{0,24},{8,32},{16,40},{24,48},{32,56},{40,64},{48,72},{56,80},{64,... | collective-permute-start | bytes 786440 | tf_op jit(solution)/shard_map/ppermute | solution.py:16
  194.0 1.8 fusion.2
  195.8 10.9 %collective-permute-done.2 = bf16[2,512,128]{2,1,0:T(8,128)(2,1)S(1)} collective-permute-done((bf16[2,512,128]{2,1,0:T(8,128)(2,1)}, bf16[2,512,128]{2,1,0:T(8,128)(2,1)S(1)}, u32[]{:S(2)}, u32[]{:S(2)}) %collective-permute-start.2) | collective-permute-done | bytes 262176 | tf_op jit(solution)/shard_map/ppermute | solution.py:16
  206.7 11.1 %collective-permute-start.3 = (bf16[2,512,128]{2,1,0:T(8,128)(2,1)}, bf16[2,512,128]{2,1,0:T(8,128)(2,1)S(1)}, u32[]{:S(2)}, u32[]{:S(2)}) collective-permute-start(bf16[2,512,128]{2,1,0:T(8,128)(2,1)} %pad_maximum_fusion), channel_id=1, source_target_pairs={{0,32},{8,40},{16,48},{24,56},{32,64},{40,72},{48,80},{56,88},{64,... | collective-permute-start | bytes 786440 | tf_op jit(solution)/shard_map/ppermute | solution.py:16
  217.8 0.9 fusion.3
  218.7 7.8 %collective-permute-done.3 = bf16[2,512,128]{2,1,0:T(8,128)(2,1)S(1)} collective-permute-done((bf16[2,512,128]{2,1,0:T(8,128)(2,1)}, bf16[2,512,128]{2,1,0:T(8,128)(2,1)S(1)}, u32[]{:S(2)}, u32[]{:S(2)}) %collective-permute-start.3) | collective-permute-done | bytes 262176 | tf_op jit(solution)/shard_map/ppermute | solution.py:16
  226.4 9.1 %collective-permute-start = (bf16[2,512,128]{2,1,0:T(8,128)(2,1)}, bf16[2,512,128]{2,1,0:T(8,128)(2,1)S(1)}, u32[]{:S(2)}, u32[]{:S(2)}) collective-permute-start(bf16[2,512,128]{2,1,0:T(8,128)(2,1)} %pad_maximum_fusion), channel_id=1, source_target_pairs={{0,8},{8,16},{16,24},{24,32},{32,40},{40,48},{48,56},{56,64},{64,7... | collective-permute-start | bytes 786440 | tf_op jit(solution)/shard_map/ppermute | solution.py:16
  235.6 0.9 fusion.4
  236.5 1.8 fusion.5
  238.3 1.8 fusion.6
  240.1 5.1 %collective-permute-done = bf16[2,512,128]{2,1,0:T(8,128)(2,1)S(1)} collective-permute-done((bf16[2,512,128]{2,1,0:T(8,128)(2,1)}, bf16[2,512,128]{2,1,0:T(8,128)(2,1)S(1)}, u32[]{:S(2)}, u32[]{:S(2)}) %collective-permute-start) | collective-permute-done | bytes 262176 | tf_op jit(solution)/shard_map/ppermute | solution.py:16
  245.3 0.9 fusion.1
  246.2 1.8 fusion.7
  248.0 1.8 fusion.8
  249.9 1.0 fusion.9
  250.9 1.0 fusion.25
  251.9 1.0 fusion.23
  253.0 1.0 fusion.21
  254.0 1.1 fusion.19
  255.1 1.0 fusion.17
  256.1 1.3 fusion.15
  257.4 1.1 fusion.13
  258.5 1.1 fusion.11
  259.6 2.1 fusion.93
  261.6 2.4 fusion.66
  264.0 2.4 fusion.69
  266.4 2.4 fusion.72
  268.9 1.5 fusion.75
  270.4 1.5 fusion.78
  271.9 2.4 fusion.81
  274.3 3.2 fusion.141
  277.5 2.9 divide_convert_fusion
  280.4 0.4 copy.108
  280.9 0.2 reshape_reshape.3
  281.1 0.6 gather_fusion
  281.8 50.9 %all_to_all.42 = bf16[64,8,512]{2,1,0:T(8,128)(2,1)S(1)} all-to-all(bf16[64,8,512]{2,1,0:T(8,128)(2,1)S(1)} %broadcast_select_fusion), channel_id=1, replica_groups=mesh['ctx'=64,'head'=8] {'ctx'}, dimensions={0} | all-to-all | bytes 1048576 | tf_op jit(solution)/shard_map/all_to_all | solution.py:117
  332.8 0.8 copy.191
  (41 shorter events, 0.8 us)
Async XLA Ops:
  0.0 0.9 copy-start
  1.6 24.3 %all-to-all-start.2 = ((bf16[64,8,128]{2,0,1:T(8,128)(2,1)}), bf16[64,8,128]{2,0,1:T(8,128)(2,1)S(1)}, u32[]{:S(2)}, u32[]{:S(2)}) async-start(bf16[64,8,128]{2,0,1:T(8,128)(2,1)} %copy_bitcast_fusion.1), calls=%async_computation.2 | async-start | bytes 262144 | tf_op jit(solution)/shard_map/all_to_all | solution.py:31
  25.9 8.2 %all-to-all-start = ((bf16[8,64,128]{2,1,0:T(8,128)(2,1)}), bf16[8,64,128]{2,1,0:T(8,128)(2,1)S(1)}, u32[]{:S(2)}, u32[]{:S(2)}) async-start(bf16[8,64,128]{2,1,0:T(8,128)(2,1)} %constant_dynamic-update-slice_fusion), calls=%async_computation | async-start | bytes 262144 | tf_op jit(solution)/shard_map/all_to_all | solution.py:28
  34.1 43.2 %all-to-all-start.1 = ((bf16[64,8,512]{2,0,1:T(8,128)(2,1)}), bf16[64,8,512]{2,0,1:T(8,128)(2,1)S(1)}, u32[]{:S(2)}, u32[]{:S(2)}) async-start(bf16[64,8,512]{2,0,1:T(8,128)(2,1)} %bitcast.471), calls=%async_computation.1 | async-start | bytes 1048576 | tf_op jit(solution)/shard_map/all_to_all | solution.py:26
  42.2 205.8 %collective-permute-start.7 = (bf16[2,512,128]{2,1,0:T(8,128)(2,1)}, bf16[2,512,128]{2,1,0:T(8,128)(2,1)}, u32[]{:S(2)}, u32[]{:S(2)}) collective-permute-start(bf16[2,512,128]{2,1,0:T(8,128)(2,1)} %pad_maximum_fusion), channel_id=1, source_target_pairs={{0,64},{8,72},{16,80},{24,88},{32,96},{40,104},{48,112},{56,120},{... | collective-permute-start | bytes 786440 | tf_op jit(solution)/shard_map/ppermute | solution.py:16
  54.3 191.9 %collective-permute-start.6 = (bf16[2,512,128]{2,1,0:T(8,128)(2,1)}, bf16[2,512,128]{2,1,0:T(8,128)(2,1)}, u32[]{:S(2)}, u32[]{:S(2)}) collective-permute-start(bf16[2,512,128]{2,1,0:T(8,128)(2,1)} %pad_maximum_fusion), channel_id=1, source_target_pairs={{0,56},{8,64},{16,72},{24,80},{32,88},{40,96},{48,104},{56,112},{6... | collective-permute-start | bytes 786440 | tf_op jit(solution)/shard_map/ppermute | solution.py:16
  60.7 177.6 %collective-permute-start.5 = (bf16[2,512,128]{2,1,0:T(8,128)(2,1)}, bf16[2,512,128]{2,1,0:T(8,128)(2,1)}, u32[]{:S(2)}, u32[]{:S(2)}) collective-permute-start(bf16[2,512,128]{2,1,0:T(8,128)(2,1)} %pad_maximum_fusion), channel_id=1, source_target_pairs={{0,48},{8,56},{16,64},{24,72},{32,80},{40,88},{48,96},{56,104},{64... | collective-permute-start | bytes 786440 | tf_op jit(solution)/shard_map/ppermute | solution.py:16
  65.3 171.1 %collective-permute-start.4 = (bf16[2,512,128]{2,1,0:T(8,128)(2,1)}, bf16[2,512,128]{2,1,0:T(8,128)(2,1)}, u32[]{:S(2)}, u32[]{:S(2)}) collective-permute-start(bf16[2,512,128]{2,1,0:T(8,128)(2,1)} %pad_maximum_fusion), channel_id=1, source_target_pairs={{0,40},{8,48},{16,56},{24,64},{32,72},{40,80},{48,88},{56,96},{64,... | collective-permute-start | bytes 786440 | tf_op jit(solution)/shard_map/ppermute | solution.py:16
  74.0 114.2 %collective-permute-start.1 = (bf16[2,512,128]{2,1,0:T(8,128)(2,1)}, bf16[2,512,128]{2,1,0:T(8,128)(2,1)}, u32[]{:S(2)}, u32[]{:S(2)}) collective-permute-start(bf16[2,512,128]{2,1,0:T(8,128)(2,1)} %pad_maximum_fusion), channel_id=1, source_target_pairs={{0,16},{8,24},{16,32},{24,40},{32,48},{40,56},{48,64},{56,72},{64,... | collective-permute-start | bytes 786440 | tf_op jit(solution)/shard_map/ppermute | solution.py:16
  188.2 18.5 %collective-permute-start.2 = (bf16[2,512,128]{2,1,0:T(8,128)(2,1)}, bf16[2,512,128]{2,1,0:T(8,128)(2,1)S(1)}, u32[]{:S(2)}, u32[]{:S(2)}) collective-permute-start(bf16[2,512,128]{2,1,0:T(8,128)(2,1)} %pad_maximum_fusion), channel_id=1, source_target_pairs={{0,24},{8,32},{16,40},{24,48},{32,56},{40,64},{48,72},{56,80},{64,... | collective-permute-start | bytes 786440 | tf_op jit(solution)/shard_map/ppermute | solution.py:16
  206.7 28.9 %copy-start.4 = (bf16[2,512,128]{2,1,0:T(8,128)(2,1)}, bf16[2,512,128]{2,1,0:T(8,128)(2,1)S(1)}, u32[]{:S(2)}) copy-start(bf16[2,512,128]{2,1,0:T(8,128)(2,1)S(1)} %collective-permute-done.2) | copy-start | bytes 786436
  206.7 19.8 %collective-permute-start.3 = (bf16[2,512,128]{2,1,0:T(8,128)(2,1)}, bf16[2,512,128]{2,1,0:T(8,128)(2,1)S(1)}, u32[]{:S(2)}, u32[]{:S(2)}) collective-permute-start(bf16[2,512,128]{2,1,0:T(8,128)(2,1)} %pad_maximum_fusion), channel_id=1, source_target_pairs={{0,32},{8,40},{16,48},{24,56},{32,64},{40,72},{48,80},{56,88},{64,... | collective-permute-start | bytes 786440 | tf_op jit(solution)/shard_map/ppermute | solution.py:16
  226.4 11.9 %copy-start.6 = (bf16[2,512,128]{2,1,0:T(8,128)(2,1)}, bf16[2,512,128]{2,1,0:T(8,128)(2,1)S(1)}, u32[]{:S(2)}) copy-start(bf16[2,512,128]{2,1,0:T(8,128)(2,1)S(1)} %collective-permute-done.3) | copy-start | bytes 786436
  226.4 18.8 %collective-permute-start = (bf16[2,512,128]{2,1,0:T(8,128)(2,1)}, bf16[2,512,128]{2,1,0:T(8,128)(2,1)S(1)}, u32[]{:S(2)}, u32[]{:S(2)}) collective-permute-start(bf16[2,512,128]{2,1,0:T(8,128)(2,1)} %pad_maximum_fusion), channel_id=1, source_target_pairs={{0,8},{8,16},{16,24},{24,32},{32,40},{40,48},{48,56},{56,64},{64,7... | collective-permute-start | bytes 786440 | tf_op jit(solution)/shard_map/ppermute | solution.py:16
  235.5 2.8 copy-start.1
  245.3 2.7 copy-start.2
  266.4 2.5 copy-start.7
  268.9 1.5 copy-start.5
  271.9 2.4 copy-start.3
